TPU v7x, 256 devices: a whole 4x4x8 slice. The times are simulated.
256 devices in a mesh: seq: 16 (over z, x_lo), wr: 4 (over y), wc: 4 (over x_hi, core).
Axes of the slice: x: 4 (x_hi: 2, x_lo: 2; x = x_hi * 2 + x_lo), y: 4, z: 8, core: 2. Of those that a mesh axis runs over, the one named last changes fastest.
Arguments:
- tokens: bfloat16 [8192, 2048], P('seq', ('wr', 'wc')), may hold values from -6 to 6
- ln_gain: float32 [2, 2048], replicated, may hold values from 0.5 to 1.5
- w_branch: bfloat16 [2, 2048, 4096], P(None, None, ('wr', 'wc')), may hold values from -0.125 to 0.125
- w_outgate: bfloat16 [2, 2048, 4096], P(None, None, ('wr', 'wc')), may hold values from -0.125 to 0.125
- w_gates: bfloat16 [2, 2048, 8], replicated, may hold values from -0.125 to 0.125
- forget_bias: float32 [2, 4], replicated, may hold values from 3.2 to 11
- conv_weight: float32 [2, 4, 4096], P(None, None, ('wr', 'wc')), may hold values from -3 to 3
- conv_bias: float32 [2, 4096], P(None, ('wr', 'wc')), may hold values from -3 to 3
- w_query: float32 [2, 4, 4, 4, 256], P(None, 'wr'), may hold values from -3 to 3
- w_key: float32 [2, 4, 4, 4, 256], P(None, 'wr'), may hold values from -3 to 3
- w_value: float32 [2, 4, 4, 4, 256], P(None, 'wr', None, 'wc'), may hold values from -4 to 4
- skip_gain: float32 [2, 4096], P(None, ('wr', 'wc')), may hold values from 0.5 to 1.5
- norm_gain: float32 [2, 4096], P(None, ('wr', 'wc')), may hold values from 0.5 to 1.5
- w_down: bfloat16 [2, 4096, 2048], P(None, ('wr', 'wc')), may hold values from -0.125 to 0.125
- lengths: int32 [3], replicated, may hold values from 1 to 4096, 8192 in all
- request_prompt: int32 [32], P('seq'), may hold values from 0 to 2
Outputs:
- mixed: bfloat16 [8192, 2048], P('seq', ('wr', 'wc'))
- request_state: bfloat16 [2, 32, 4, 1024, 1024], P(None, 'seq', 'wr', None, 'wc')
- request_conv: bfloat16 [2, 32, 3, 4096], P(None, 'seq', None, ('wr', 'wc'))
Inputs may be any that keep to these rules, and one draw needn't show every extreme that they name: `lengths`: the 3 prompts lie end to end in order and fill all 8192 positions; the longest has exactly 4096 positions.
All inputs are finite; a program needn't handle non-finite values.
Results may differ from a plain program's by a relative error of at most 0.035.
Values may be sent and summed in bfloat16 or wider, within the bound.
A program may use at most 128 MiB of HBM per device.

v0:
```python
import jax
import jax.numpy as jnp
from jax import lax
from jax.sharding import PartitionSpec as P

HEADS = 4
CONV = 4
LAYERS = 2
PROMPTS = 3
EPSILON = 1e-05
GATE_CAP = 15.0
ROW_DIMS = (((0,), (0,)), ((), ()))
FEATURE_DIMS = (((1,), (1,)), ((), ()))


def shifted(value, axis, steps):
    count = lax.axis_size(axis)
    first, last = (max(0, -steps), min(count, count - steps))
    return lax.ppermute(value, axis, [(source, source + steps) for source in range(first, last)])


def entering_2(shard, axis, join, neutral):
    place = lax.axis_index(axis)
    gathered = jax.tree.map(
        lambda a, kind: lax.all_gather(a.astype(kind), axis), shard, (jnp.bfloat16, jnp.bfloat16)
    )
    state = jax.tree.map(lambda a, e: jnp.zeros_like(a) + jnp.asarray(e, a.dtype), shard, neutral)

    def one(step, state):
        return join(
            state,
            jax.tree.map(
                lambda a, own: lax.dynamic_index_in_dim(a, step, 0, False).astype(own.dtype),
                gathered,
                shard,
            ),
        )

    return lax.fori_loop(0, place, one, state)


def broadcast(shard, axis, root):
    mine = lax.axis_index(axis) == root
    return lax.psum(jnp.where(mine, shard, jnp.zeros_like(shard)), axis)


def norm_rows(source, gain_row):
    widened = source.astype(jnp.float32)
    row_mean = jnp.mean(widened, axis=1, keepdims=True)
    row_var = jnp.mean(widened * widened, axis=1, keepdims=True) - row_mean * row_mean
    return ((widened - row_mean) * lax.rsqrt(row_var + EPSILON) * gain_row).astype(jnp.bfloat16)


def segment_of(positions, lengths):
    bound_one = lengths[0]
    bound_two = lengths[0] + lengths[1]
    return (positions >= bound_one).astype(jnp.int32) + (positions >= bound_two).astype(jnp.int32)


def conv_rows(extended, ext_segment, segment, weight, bias_row):
    row_count = segment.shape[0]
    widened = extended.astype(jnp.float32)
    summed = jnp.zeros((row_count, widened.shape[1]), jnp.float32) + bias_row
    for back_step in range(weight.shape[0]):
        low_row = weight.shape[0] - 1 - back_step
        keep_row = (ext_segment[low_row : low_row + row_count] == segment).astype(jnp.float32)
        summed = (
            summed + weight[back_step] * widened[low_row : low_row + row_count] * keep_row[:, None]
        )
    return jax.nn.silu(summed).astype(jnp.bfloat16)


def block_mix(source, weight):
    row_count = source.shape[0]
    grouped = source.astype(jnp.float32).reshape(row_count, 4, -1)
    mixed = jnp.einsum("tig,ijg->tjg", grouped, weight, precision=lax.Precision.HIGHEST)
    return mixed.reshape(row_count, -1)


def block_terms(queries, key_rows, values, log_forget, in_gate, segment, prev_seg):
    row_count = queries.shape[0]
    cum_log = jnp.cumsum(log_forget)
    row_order = jnp.arange(row_count)
    allowed = (row_order[:, None] >= row_order[None, :]) & (segment[:, None] == segment[None, :])
    exponent = jnp.where(allowed, cum_log[:, None] - cum_log[None, :] + in_gate[None, :], -jnp.inf)
    scores = lax.dot_general(
        queries, key_rows, FEATURE_DIMS, preferred_element_type=jnp.float32
    ) * jnp.exp(exponent)
    in_block = jnp.dot(scores.astype(jnp.bfloat16), values, preferred_element_type=jnp.float32)
    carried = jnp.where(segment == prev_seg, jnp.exp(cum_log), 0.0)
    last_seg = segment[row_count - 1]
    weights = jnp.where(
        segment == last_seg, jnp.exp(cum_log[row_count - 1] - cum_log + in_gate), 0.0
    )
    weighted = (key_rows.astype(jnp.float32) * weights[:, None]).astype(jnp.bfloat16)
    increment = lax.dot_general(weighted, values, ROW_DIMS, preferred_element_type=jnp.float32)
    block_decay = jnp.where(last_seg == prev_seg, jnp.exp(cum_log[row_count - 1]), 0.0)
    return (in_block, carried, increment, block_decay)


def end_state(
    state_in, key_rows, values, cum_log, in_gate, segment, seg_before, local_end, prompt, holder
):
    end_cum = cum_log[local_end]
    entering = jnp.where(holder & (seg_before == prompt), jnp.exp(end_cum), 0.0)
    row_order = jnp.arange(segment.shape[0])
    chosen = holder & (segment == prompt) & (row_order <= local_end)
    weights = jnp.where(chosen, jnp.exp(end_cum - cum_log + in_gate), 0.0)
    weighted = (key_rows.astype(jnp.float32) * weights[:, None]).astype(jnp.bfloat16)
    return entering * state_in + lax.dot_general(
        weighted, values, ROW_DIMS, preferred_element_type=jnp.float32
    )


def combine_states(earlier, later):
    return (earlier[0] * later[0], later[0] * earlier[1] + later[1])


def body(
    tokens,
    ln_gain,
    w_branch,
    w_outgate,
    w_gates,
    forget_bias,
    conv_weight,
    conv_bias,
    w_query,
    w_key,
    w_value,
    skip_gain,
    norm_gain,
    w_down,
    lengths,
    request_prompt,
):
    tok_rows = tokens.shape[0]
    seq_count = lax.axis_size("seq")
    seq_index = lax.axis_index("seq")
    head_idx = lax.axis_index("wr")
    row_offset = seq_index * tok_rows
    total_rows = tok_rows * seq_count
    row_ids = jnp.arange(tok_rows, dtype=jnp.int32)
    positions = row_offset + row_ids
    segment = segment_of(positions, lengths)
    seg_before = jnp.where(row_offset > 0, segment_of(row_offset - 1, lengths), -1)
    rim_positions = row_offset - (CONV - 1) + jnp.arange(CONV - 1, dtype=jnp.int32)
    rim_segment = jnp.where(rim_positions >= 0, segment_of(rim_positions, lengths), -1)
    ext_segment = jnp.concatenate([rim_segment, segment])
    prompt_starts = [jnp.zeros((), jnp.int32), lengths[0], lengths[0] + lengths[1]]
    prompt_ends = [
        lengths[0] - 1,
        lengths[0] + lengths[1] - 1,
        jnp.zeros((), jnp.int32) + (total_rows - 1),
    ]
    head_mask = (jnp.arange(HEADS, dtype=jnp.int32) == head_idx).astype(jnp.float32)
    current = tokens
    sent_states = []
    sent_edges = []
    for layer_idx in range(LAYERS):
        gathered = lax.all_gather(current, ("wr", "wc"), axis=1, tiled=True)
        normed = norm_rows(gathered, ln_gain[layer_idx])
        branch = jnp.dot(normed, w_branch[layer_idx], preferred_element_type=jnp.float32).astype(
            jnp.bfloat16
        )
        outgate = jnp.dot(normed, w_outgate[layer_idx], preferred_element_type=jnp.float32)
        gate_pre = jnp.dot(normed, w_gates[layer_idx], preferred_element_type=jnp.float32)
        input_pre = jnp.sum(gate_pre[:, :HEADS] * head_mask, axis=1)
        forget_pre = jnp.sum((gate_pre[:, HEADS:] + forget_bias[layer_idx]) * head_mask, axis=1)
        in_gate = GATE_CAP * jnp.tanh(input_pre / GATE_CAP)
        log_forget = jax.nn.log_sigmoid(forget_pre)
        edge_in = shifted(branch[tok_rows - (CONV - 1) :], "seq", 1)
        extended = jnp.concatenate([edge_in, branch], axis=0)
        conv_act = conv_rows(
            extended, ext_segment, segment, conv_weight[layer_idx], conv_bias[layer_idx]
        )
        head_branch, head_act = (
            lax.all_gather(branch, "wc", axis=1, tiled=True),
            lax.all_gather(conv_act, "wc", axis=1, tiled=True),
        )
        head_width = head_act.shape[1]
        queries = block_mix(head_act, w_query[layer_idx, 0]).astype(jnp.bfloat16)
        key_rows = (block_mix(head_act, w_key[layer_idx, 0]) * head_width ** (-0.5)).astype(
            jnp.bfloat16
        )
        values = block_mix(head_branch, w_value[layer_idx, 0]).astype(jnp.bfloat16)
        prefix = jnp.zeros((head_width, values.shape[1]), jnp.float32)
        reach_all = jnp.ones((), jnp.float32)
        in_block, carried, increment, block_decay = block_terms(
            queries, key_rows, values, log_forget, in_gate, segment, seg_before
        )
        saved_parts = (in_block, carried, reach_all, prefix)
        prefix = block_decay * prefix + increment
        reach_all = block_decay * reach_all
        entering = entering_2(
            (reach_all, prefix),
            "seq",
            combine_states,
            (jnp.ones((), jnp.float32), jnp.zeros_like(prefix)),
        )[1]
        in_block, carried, reach_here, prefix_here = saved_parts
        state_here = (reach_here * entering + prefix_here).astype(jnp.bfloat16)
        hidden_parts = in_block + carried[:, None] * jnp.dot(
            queries, state_here, preferred_element_type=jnp.float32
        )
        sums_one, sums_two = lax.psum(
            (jnp.sum(hidden_parts, axis=1), jnp.sum(hidden_parts * hidden_parts, axis=1)), "wc"
        )
        row_mean = sums_one / head_width
        row_var = sums_two / head_width - row_mean * row_mean
        normal_rows = (hidden_parts - row_mean[:, None]) * lax.rsqrt(row_var + EPSILON)[:, None]
        gated = (
            (
                normal_rows * norm_gain[layer_idx]
                + skip_gain[layer_idx] * conv_act.astype(jnp.float32)
            )
            * jax.nn.silu(outgate)
        ).astype(jnp.bfloat16)
        term_rows = jnp.dot(gated, w_down[layer_idx], preferred_element_type=jnp.float32)
        summed = lax.psum_scatter(
            term_rows.astype(jnp.bfloat16), ("wr", "wc"), scatter_dimension=1, tiled=True
        ).astype(jnp.float32)
        current = (current.astype(jnp.float32) + summed).astype(jnp.bfloat16)
        cum_log = jnp.cumsum(log_forget)
        for prompt in range(PROMPTS):
            end_pos = prompt_ends[prompt]
            holder = (end_pos >= row_offset) & (end_pos < row_offset + tok_rows)
            local_end = jnp.clip(end_pos - row_offset, 0, tok_rows - 1)
            state_end = end_state(
                entering,
                key_rows,
                values,
                cum_log,
                in_gate,
                segment,
                seg_before,
                local_end,
                prompt,
                holder,
            )
            window = lax.dynamic_slice_in_dim(extended, local_end + 1, CONV - 1, 0)
            edge_pos = end_pos - (CONV - 2) + jnp.arange(CONV - 1, dtype=jnp.int32)
            edge_rows = jnp.where(
                ((edge_pos >= prompt_starts[prompt]) & holder)[:, None],
                window,
                jnp.zeros_like(window),
            )
            got_state, got_edge = (
                broadcast(state_end.astype(jnp.bfloat16), "seq", end_pos // tok_rows),
                broadcast(edge_rows, "seq", end_pos // tok_rows),
            )
            sent_states.append(got_state)
            sent_edges.append(got_edge)
    state_stack = jnp.stack(sent_states)
    edge_stack = jnp.stack(sent_edges)
    state_stack = state_stack.reshape(LAYERS, PROMPTS, state_stack.shape[1], state_stack.shape[2])
    edge_stack = edge_stack.reshape(LAYERS, PROMPTS, edge_stack.shape[1], edge_stack.shape[2])
    chooser = (request_prompt[:, None] == jnp.arange(PROMPTS, dtype=jnp.int32)[None, :]).astype(
        jnp.bfloat16
    )
    request_state = jnp.einsum(
        "rp,lphd->lrhd", chooser, state_stack, preferred_element_type=jnp.float32
    ).astype(jnp.bfloat16)[:, :, None]
    request_conv = jnp.einsum(
        "rp,lpkc->lrkc", chooser, edge_stack, preferred_element_type=jnp.float32
    ).astype(jnp.bfloat16)
    return (current, request_state, request_conv)


def solution(mesh):
    return jax.shard_map(
        body,
        mesh=mesh,
        in_specs=(
            P("seq", ("wr", "wc")),
            P(),
            P(None, None, ("wr", "wc")),
            P(None, None, ("wr", "wc")),
            P(),
            P(),
            P(None, None, ("wr", "wc")),
            P(None, ("wr", "wc")),
            P(None, "wr", None, None, None),
            P(None, "wr", None, None, None),
            P(None, "wr", None, "wc", None),
            P(None, ("wr", "wc")),
            P(None, ("wr", "wc")),
            P(None, ("wr", "wc"), None),
            P(),
            P("seq"),
        ),
        out_specs=(
            P("seq", ("wr", "wc")),
            P(None, "seq", "wr", None, "wc"),
            P(None, "seq", None, ("wr", "wc")),
        ),
        check_vma=False,
    )
```

profile of v0, /device:TPU:8, one launch (start us, length us, event | category | flops | bytes accessed | tf_op | source)
XLA Modules:
  0.0 1085.9 jit_solution(4009449505985787538)
XLA Ops:
  17.0 47.1 %all-gather.11.cloned.1.call-done = bf16[512,2048]{1,0:T(8,128)(2,1)} async-done(((bf16[512,128]{1,0:T(8,128)(2,1)}), bf16[512,2048]{1,0:T(8,128)(2,1)}) %all-gather.11.cloned.1.call-update) | async-done | bytes 2097168 | tf_op jit(solution)/shard_map/all_gather | solution.py:161
  83.8 8.9 all-gather.15.cloned.1.call-done
  97.7 19.7 %all-gather.13.cloned.1.call-done = bf16[512,1024]{1,0:T(8,128)(2,1)} async-done(((bf16[512,256]{1,0:T(8,128)(2,1)}), bf16[512,1024]{1,0:T(8,128)(2,1)}) %all-gather.13.cloned.1.call-update) | async-done | bytes 1048592 | tf_op jit(solution)/shard_map/all_gather | solution.py:179
  122.8 4.2 fusion.99
  144.2 38.1 %all-reduce = bf16[16]{0:T(256)(128)(2,1)S(1)} all-reduce(bf16[16]{0:T(256)(128)(2,1)} %dynamic-update-slice), channel_id=1, replica_groups=mesh['seq'=16,'wr'=4,'wc'=4] {'seq'}, use_global_device_ids=true, to_apply=%add | all-reduce | flops 16 | bytes 64
  187.8 3.2 fusion.53
  191.0 130.3 %all-gather.23.cloned.1.call-done = bf16[16384,256]{1,0:T(8,128)(2,1)} async-done(((bf16[1024,256]{1,0:T(8,128)(2,1)}), bf16[16384,256]{1,0:T(8,128)(2,1)}) %all-gather.23.cloned.1.call-update) | async-done | bytes 8388624 | tf_op jit(solution)/shard_map/all_gather | solution.py:25
  324.8 9.4 all-reduce.3
  334.9 5.5 convolution_convert_fusion.1
  340.4 3.9 copy.136
  344.4 114.9 %reduce-scatter.7.cloned.1.call-done = bf16[128,512]{1,0:T(8,128)(2,1)} async-done(((bf16[2048,512]{1,0:T(8,128)(2,1)}), bf16[128,512]{1,0:T(8,128)(2,1)}) %reduce-scatter.7.cloned.1.call-update) | async-done | bytes 131088
  461.1 51.2 %all-gather.17.cloned.1.call-done = bf16[512,2048]{1,0:T(8,128)(2,1)} async-done(((bf16[512,128]{1,0:T(8,128)(2,1)}), bf16[512,2048]{1,0:T(8,128)(2,1)}) %all-gather.17.cloned.1.call-update) | async-done | bytes 2097168 | tf_op jit(solution)/shard_map/all_gather | solution.py:161
  532.5 8.4 all-gather.21.cloned.1.call-done
  545.0 20.6 %all-gather.19.cloned.1.call-done = bf16[512,1024]{1,0:T(8,128)(2,1)} async-done(((bf16[512,256]{1,0:T(8,128)(2,1)}), bf16[512,1024]{1,0:T(8,128)(2,1)}) %all-gather.19.cloned.1.call-update) | async-done | bytes 1048592 | tf_op jit(solution)/shard_map/all_gather | solution.py:179
  568.9 4.2 fusion.96
  590.7 71.5 %all-reduce.4 = (bf16[16]{0:T(256)(128)(2,1)S(1)}, bf16[1,3,256]{2,1,0:T(4,128)(2,1)S(1)}, bf16[1,3,256]{2,1,0:T(4,128)(2,1)S(1)}, bf16[1,3,256]{2,1,0:T(4,128)(...) all-reduce(bf16[16]{0:T(256)(128)(2,1)S(1)} %dynamic-update-slice.1, ...), channel_id=1, replica_groups=mesh['seq'=16,'wr'=4,'wc'=4] {'seq'}, use_global_device_ids=true, to_apply=%add.1 | all-reduce | flops 4624 | bytes 18496
  667.5 3.3 fusion.52
  670.8 99.3 %all-gather.25.cloned.1.call-done = bf16[16384,256]{1,0:T(8,128)(2,1)} async-done(((bf16[1024,256]{1,0:T(8,128)(2,1)}), bf16[16384,256]{1,0:T(8,128)(2,1)}) %all-gather.25.cloned.1.call-update) | async-done | bytes 8388624 | tf_op jit(solution)/shard_map/all_gather | solution.py:25
  773.1 8.8 all-reduce.2
  782.0 6.1 convolution_convert_fusion
  788.1 3.9 copy.138
  798.1 3.4 fusion.19
  823.8 82.0 %reduce-scatter.9.cloned.1.call-done = bf16[128,512]{1,0:T(8,128)(2,1)} async-done(((bf16[2048,512]{1,0:T(8,128)(2,1)}), bf16[128,512]{1,0:T(8,128)(2,1)}) %reduce-scatter.9.cloned.1.call-update) | async-done | bytes 131088
  907.5 164.3 %all-reduce.8.cloned.1.call-done = (bf16[1,1024,256]{2,1,0:T(8,128)(2,1)}, bf16[1,1024,256]{2,1,0:T(8,128)(2,1)}, bf16[1,1024,256]{2,1,0:T(8,128)(2,1)}, bf16[1,...) async-done(((bf16[1,1024,256]{2,1,0:T(8,128)(2,1)}, bf16[1,1024,256]{2,1,0:T(8,128)(2,1)}, bf16[1,1024,256]{2,1,0:T(8,128)(2,1)}, ...) | async-done | bytes 3145744 | tf_op jit(solution)/shard_map/psum | solution.py:44
  (254 shorter events, 149.1 us)
Async XLA Ops:
  7.2 56.9 %all-gather.11.cloned.1.call-start = ((), (), s32[]{:S(2)}) async-start(), calls=%async_computation.2 | async-start | bytes 2228224 | tf_op jit(solution)/shard_map/all_gather | solution.py:161
  7.9 84.8 %all-gather.15.cloned.1.call-start = ((), (), s32[]{:S(2)}) async-start(), calls=%async_computation.4 | async-start | bytes 1310720 | tf_op jit(solution)/shard_map/all_gather | solution.py:178
  11.3 59.7 %copy-start.39 = (f32[4]{0:T(128)}, f32[4]{0:T(128)S(1)}, u32[]{:S(2)}) copy-start(f32[4]{0:T(128)S(1)} %compare_convert_fusion) | copy-start | bytes 52
  69.6 47.8 %all-gather.13.cloned.1.call-start = ((), (), s32[]{:S(2)}) async-start(), calls=%async_computation.3 | async-start | bytes 1310720 | tf_op jit(solution)/shard_map/all_gather | solution.py:179
  71.0 7.3 copy-start.23
  71.1 10.8 copy-start.24
  71.5 4.1 collective-permute-start
  75.5 8.3 copy-start.30
  75.7 8.1 copy-start.27
  76.9 244.4 %all-gather.23.cloned.1.call-start = ((), (), s32[]{:S(2)}) async-start(), calls=%async_computation.8 | async-start | bytes 8912896 | tf_op jit(solution)/shard_map/all_gather | solution.py:25
  138.0 321.3 %reduce-scatter.7.cloned.1.call-start = ((), (), s32[]{:S(2)}) async-start(), calls=%async_computation.10 | async-start | bytes 2228224
  344.3 116.0 %copy-start.17 = (bf16[512,128]{1,0:T(8,128)(2,1)S(1)}, bf16[512,128]{1,0:T(8,128)(2,1)}, u32[]{:S(2)}) copy-start(bf16[512,128]{1,0:T(8,128)(2,1)} %param.20) | copy-start | bytes 393220
  344.3 168.0 %all-gather.17.cloned.1.call-start = ((), (), s32[]{:S(2)}) async-start(), calls=%async_computation.5 | async-start | bytes 2228224 | tf_op jit(solution)/shard_map/all_gather | solution.py:161
  461.0 79.9 %all-gather.21.cloned.1.call-start = ((), (), s32[]{:S(2)}) async-start(), calls=%async_computation.7 | async-start | bytes 1310720 | tf_op jit(solution)/shard_map/all_gather | solution.py:178
  516.4 10.1 copy-start
  517.8 7.6 copy-start.26
  517.8 47.8 %all-gather.19.cloned.1.call-start = ((), (), s32[]{:S(2)}) async-start(), calls=%async_computation.6 | async-start | bytes 1310720 | tf_op jit(solution)/shard_map/all_gather | solution.py:179
  518.6 3.8 collective-permute-start.1
  525.2 244.9 %all-gather.25.cloned.1.call-start = ((), (), s32[]{:S(2)}) async-start(), calls=%async_computation.9 | async-start | bytes 8912896 | tf_op jit(solution)/shard_map/all_gather | solution.py:25
  585.6 320.2 %reduce-scatter.9.cloned.1.call-start = ((), (), s32[]{:S(2)}) async-start(), calls=%async_computation.11 | async-start | bytes 2228224
  770.4 11.5 %copy-start.44 = (f32[1,256]{1,0:T(1,128)S(1)}, f32[1,256]{1,0:T(1,128)}, u32[]{:S(2)}) copy-start(f32[1,256]{1,0:T(1,128)} %get-tuple-element.222) | copy-start | bytes 3076
  770.4 11.5 %copy-start.45 = (f32[1,256]{1,0:T(1,128)S(1)}, f32[1,256]{1,0:T(1,128)}, u32[]{:S(2)}) copy-start(f32[1,256]{1,0:T(1,128)} %get-tuple-element.220) | copy-start | bytes 3076
  792.0 279.8 %all-reduce.8.cloned.1.call-start = ((), (), s32[]{:S(2)}) async-start(), calls=%async_computation.12 | async-start | bytes 6291456 | tf_op jit(solution)/shard_map/psum | solution.py:44
  822.3 84.5 %copy-start.16 = (bf16[512,128]{1,0:T(8,128)(2,1)S(1)}, bf16[512,128]{1,0:T(8,128)(2,1)}, u32[]{:S(2)}) copy-start(bf16[512,128]{1,0:T(8,128)(2,1)} %add_convert_fusion.1) | copy-start | bytes 393220
  (39 other events, 125.7 us)
Sparse Core Ops, SparseCore 0:
  10.6 53.4 all-gather.10
  69.7 22.9 all-gather.14
  94.5 22.8 all-gather.12
  138.1 183.1 all-gather.22
  344.4 114.8 reduce-scatter.6
  462.3 49.9 all-gather.16
  518.0 22.8 all-gather.20
  542.7 22.8 all-gather.18
  585.7 184.3 all-gather.24
  792.1 113.6 reduce-scatter.8
  908.9 162.8 all-reduce.7
where the time goes:
time: 1100 us; the launch traced here: 1090 us
  waiting for transfers between devices  749 us (68%)
  blocking collectives  128 us (12%)
  local copies, waits for them, and re-layouts  79.5 us (7%)
  matrix products  59.7 us (5%)
  other arithmetic  39.7 us (4%)
  between operations  24.4 us (2%)
    all_gather x2, waiting for transfers between devices, entering_2(): lax.all_gather(a.astype(kind), axis)  230 us
    unnamed x13, waiting for transfers between devices  198 us
    psum x1, waiting for transfers between devices, broadcast(): return lax.psum(jnp.where(mine, shard, jnp.zeros_like(shard)), axis)  164 us
    unnamed x2, blocking collectives  110 us
    all_gather x2, waiting for transfers between devices, body(): gathered = lax.all_gather(current, ('wr', 'wc'), axis=1, tiled=True)  98.3 us
    all_gather x2, waiting for transfers between devices, body(): lax.all_gather(conv_act, 'wc', axis=1, tiled=True)  40.3 us
    unnamed x126, local copies, waits for them, and re-layouts  27.7 us
  transfers between devices with their start and end apart: 13, of which 12 were waited for; matrix products, arithmetic and copies ran while one was open for 8% of the time, Pallas kernels for 0%

commit v1 on v0

--- a/solution.py
+++ b/solution.py
@@ -158,7 +158,10 @@
     sent_states = []
     sent_edges = []
     for layer_idx in range(LAYERS):
-        gathered = lax.all_gather(current, ("wr", "wc"), axis=1, tiled=True)
+        gathered = jnp.concatenate(
+            lax.all_to_all(jnp.stack([current] * lax.axis_size(("wr", "wc"))), ("wr", "wc"), 0, 0),
+            axis=1,
+        )
         normed = norm_rows(gathered, ln_gain[layer_idx])
         branch = jnp.dot(normed, w_branch[layer_idx], preferred_element_type=jnp.float32).astype(
             jnp.bfloat16

time: 1100 us -> 1050 us (0.955)
  waiting for transfers between devices: 749 us -> 669 us
  blocking collectives: 128 us -> 159 us
    all_gather x2 -> x0, waiting for transfers between devices: 98.3 us -> none  [body(): gathered = lax.all_gather(current, ('wr', 'wc'), axis=1, tiled=True)]
    all_to_all x0 -> x1, blocking collectives: none -> 31.8 us  [body(): lax.all_to_all(jnp.stack([current] * lax.axis_size(('wr', 'wc'))), ('wr',...]
    all_to_all x0 -> x1, waiting for transfers between devices: none -> 20.9 us  [body(): lax.all_to_all(jnp.stack([current] * lax.axis_size(('wr', 'wc'))), ('wr',...]
    unnamed x126 -> x173, local copies, waits for them, and re-layouts: 27.7 us -> 31.2 us
    unnamed x13 -> x11, waiting for transfers between devices: 198 us -> 199 us
  transfers between devices with their start and end apart: 13 -> 12, of which waited for: 12 -> 12; matrix products, arithmetic and copies ran while one was open for 8% -> 9% of each run, Pallas kernels for 0% -> 0%
where the time goes in v1:
time: 1050 us; the launch traced here: 1040 us
  waiting for transfers between devices  669 us (64%)
  blocking collectives  159 us (15%)
  local copies, waits for them, and re-layouts  75.9 us (7%)
  matrix products  59.2 us (6%)
  other arithmetic  34.9 us (3%)
  between operations  24.3 us (2%)
  starting transfers between devices  14.3 us (1%)
    all_gather x2, waiting for transfers between devices, entering_2(): lax.all_gather(a.astype(kind), axis)  232 us
    unnamed x11, waiting for transfers between devices  199 us
    psum x1, waiting for transfers between devices, broadcast(): return lax.psum(jnp.where(mine, shard, jnp.zeros_like(shard)), axis)  164 us
    unnamed x2, blocking collectives  110 us
    all_gather x2, waiting for transfers between devices, body(): lax.all_gather(conv_act, 'wc', axis=1, tiled=True)  41.7 us
    all_to_all x1, blocking collectives, body(): lax.all_to_all(jnp.stack([current] * lax.axis_size(('wr', 'wc'))), ('wr',...  31.8 us
    unnamed x173, local copies, waits for them, and re-layouts  31.2 us
  transfers between devices with their start and end apart: 12, of which 12 were waited for; matrix products, arithmetic and copies ran while one was open for 9% of the time, Pallas kernels for 0%

profile of v1, /device:TPU:8, one launch (start us, length us, event | category | flops | bytes accessed | tf_op | source)
XLA Modules:
  0.0 1037.3 jit_solution(14330611421056700775)
XLA Ops:
  9.7 7.5 all-to-all-start
  23.0 20.9 %all-to-all-done = bf16[16,512,128]{1,2,0:T(8,128)(2,1)S(1)} async-done(((bf16[16,512,128]{1,2,0:T(8,128)(2,1)}), bf16[16,512,128]{1,2,0:T(8,128)(2,1)S(1)}, u32[]{:S(2)}, u32[]{:S(2)}) %all-to-all-start) | async-done | bytes 2097184 | tf_op jit(solution)/shard_map/all_to_all | solution.py:162
  51.3 3.7 collective-permute-start
  64.5 8.3 all-gather.11.cloned.1.call-done
  76.2 21.3 %all-gather.9.cloned.1.call-done = bf16[512,1024]{1,0:T(8,128)(2,1)} async-done(((bf16[512,256]{1,0:T(8,128)(2,1)}), bf16[512,1024]{1,0:T(8,128)(2,1)}) %all-gather.9.cloned.1.call-update) | async-done | bytes 1048592 | tf_op jit(solution)/shard_map/all_gather | solution.py:182
  115.0 39.9 %all-reduce = bf16[16]{0:T(256)(128)(2,1)S(1)} all-reduce(bf16[16]{0:T(256)(128)(2,1)S(1)} %dynamic-update-slice), channel_id=1, replica_groups=mesh['seq'=16,'wr'=4,'wc'=4] {'seq'}, use_global_device_ids=true, to_apply=%add | all-reduce | flops 16 | bytes 64
  160.9 133.5 %all-gather.17.cloned.1.call-done = bf16[16384,256]{1,0:T(8,128)(2,1)} async-done(((bf16[1024,256]{1,0:T(8,128)(2,1)}), bf16[16384,256]{1,0:T(8,128)(2,1)}) %all-gather.17.cloned.1.call-update) | async-done | bytes 8388624 | tf_op jit(solution)/shard_map/all_gather | solution.py:25
  297.3 8.8 all-reduce.3
  306.2 5.5 convolution_convert_fusion.1
  311.7 3.9 copy.142
  315.7 116.1 %reduce-scatter.7.cloned.1.call-done = bf16[128,512]{1,0:T(8,128)(2,1)} async-done(((bf16[2048,512]{1,0:T(8,128)(2,1)}), bf16[128,512]{1,0:T(8,128)(2,1)}) %reduce-scatter.7.cloned.1.call-update) | async-done | bytes 131088
  433.1 31.8 %all_to_all.10 = bf16[16,512,128]{1,2,0:T(8,128)(2,1)S(1)} all-to-all(bf16[16,512,128]{1,2,0:T(8,128)(2,1)S(1)} %stack.33), channel_id=1, replica_groups=mesh['seq'=16,'wr'=4,'wc'=4] {'wr','wc'}, dimensions={0} | all-to-all | bytes 4194304 | tf_op jit(solution)/shard_map/all_to_all | solution.py:162
  484.4 4.3 exponential_select_fusion.1
  495.3 20.4 %all-gather.13.cloned.1.call-done = bf16[512,1024]{1,0:T(8,128)(2,1)} async-done(((bf16[512,256]{1,0:T(8,128)(2,1)}), bf16[512,1024]{1,0:T(8,128)(2,1)}) %all-gather.13.cloned.1.call-update) | async-done | bytes 1048592 | tf_op jit(solution)/shard_map/all_gather | solution.py:182
  519.0 4.3 fusion.96
  543.7 69.7 %all-reduce.4 = (bf16[16]{0:T(256)(128)(2,1)}, bf16[1,3,256]{2,1,0:T(4,128)(2,1)}, bf16[1,3,256]{2,1,0:T(4,128)(2,1)}, bf16[1,3,256]{2,1,0:T(4,128)(2,1)}, bf16[...) all-reduce(bf16[16]{0:T(256)(128)(2,1)} %dynamic-update-slice.1, ...), channel_id=1, replica_groups=mesh['seq'=16,'wr'=4,'wc'=4] {'seq'}, use_global_device_ids=true, to_apply=%add.1 | all-reduce | flops 4624 | bytes 18496
  618.8 3.3 fusion.52
  622.1 98.3 %all-gather.19.cloned.1.call-done = bf16[16384,256]{1,0:T(8,128)(2,1)} async-done(((bf16[1024,256]{1,0:T(8,128)(2,1)}), bf16[16384,256]{1,0:T(8,128)(2,1)}) %all-gather.19.cloned.1.call-update) | async-done | bytes 8388624 | tf_op jit(solution)/shard_map/all_gather | solution.py:25
  723.8 9.0 all-reduce.2
  732.8 6.1 convolution_convert_fusion
  738.9 3.9 copy.144
  749.3 3.4 fusion.19
  775.1 82.7 %reduce-scatter.9.cloned.1.call-done = bf16[128,512]{1,0:T(8,128)(2,1)} async-done(((bf16[2048,512]{1,0:T(8,128)(2,1)}), bf16[128,512]{1,0:T(8,128)(2,1)}) %reduce-scatter.9.cloned.1.call-update) | async-done | bytes 131088
  859.5 163.8 %all-reduce.8.cloned.1.call-done = (bf16[1,1024,256]{2,1,0:T(8,128)(2,1)}, bf16[1,1024,256]{2,1,0:T(8,128)(2,1)}, bf16[1,1024,256]{2,1,0:T(8,128)(2,1)}, bf16[1,...) async-done(((bf16[1,1024,256]{2,1,0:T(8,128)(2,1)}, bf16[1,1024,256]{2,1,0:T(8,128)(2,1)}, bf16[1,1024,256]{2,1,0:T(8,128)(2,1)}, ...) | async-done | bytes 3145744 | tf_op jit(solution)/shard_map/psum | solution.py:44
  (301 shorter events, 142.8 us)
Async XLA Ops:
  9.7 12.1 %copy-start.43 = (f32[2,4,256]{2,1,0:T(4,128)S(1)}, f32[2,4,256]{2,1,0:T(4,128)}, u32[]{:S(2)}) copy-start(f32[2,4,256]{2,1,0:T(4,128)} %param.26) | copy-start | bytes 24580
  9.7 12.7 %copy-start.36 = (f32[2,2048]{1,0:T(2,128)S(1)}, f32[2,2048]{1,0:T(2,128)}, u32[]{:S(2)}) copy-start(f32[2,2048]{1,0:T(2,128)} %param.21) | copy-start | bytes 49156
  9.7 34.2 %all-to-all-start = ((bf16[16,512,128]{1,2,0:T(8,128)(2,1)}), bf16[16,512,128]{1,2,0:T(8,128)(2,1)S(1)}, u32[]{:S(2)}, u32[]{:S(2)}) async-start(bf16[16,512,128]{1,2,0:T(8,128)(2,1)} %stack.32), calls=%async_computation | async-start | bytes 4194304 | tf_op jit(solution)/shard_map/all_to_all | solution.py:162
  17.3 55.5 %all-gather.11.cloned.1.call-start = ((), (), s32[]{:S(2)}) async-start(), calls=%async_computation.5 | async-start | bytes 1310720 | tf_op jit(solution)/shard_map/all_gather | solution.py:181
  20.0 30.8 %copy-start.51 = (f32[4]{0:T(128)}, f32[4]{0:T(128)S(1)}, u32[]{:S(2)}) copy-start(f32[4]{0:T(128)S(1)} %compare_convert_fusion) | copy-start | bytes 52
  48.0 49.5 %all-gather.9.cloned.1.call-start = ((), (), s32[]{:S(2)}) async-start(), calls=%async_computation.4 | async-start | bytes 1310720 | tf_op jit(solution)/shard_map/all_gather | solution.py:182
  50.9 12.3 %copy-start.31 = (f32[512]{0:T(512)}, f32[512]{0:T(512)S(1)}, u32[]{:S(2)}) copy-start(f32[512]{0:T(512)S(1)} %get-tuple-element.116) | copy-start | bytes 6148
  51.3 5.0 collective-permute-start
  55.9 103.0 %copy-start.24 = (f32[512]{0:T(512)}, f32[512]{0:T(512)S(1)}, u32[]{:S(2)}) copy-start(f32[512]{0:T(512)S(1)} %get-tuple-element.165) | copy-start | bytes 6148
  55.9 103.0 %copy-start.45 = (s32[512]{0:T(512)}, s32[512]{0:T(512)S(1)}, u32[]{:S(2)}) copy-start(s32[512]{0:T(512)S(1)} %convert_add_fusion.2) | copy-start | bytes 6148
  57.5 236.9 %all-gather.17.cloned.1.call-start = ((), (), s32[]{:S(2)}) async-start(), calls=%async_computation.8 | async-start | bytes 8912896 | tf_op jit(solution)/shard_map/all_gather | solution.py:25
  107.4 51.6 %copy-start.4 = (bf16[512,4,256]{2,0,1:T(8,128)(2,1)}, bf16[512,4,256]{2,0,1:T(8,128)(2,1)S(1)}, u32[]{:S(2)}) copy-start(bf16[512,4,256]{2,0,1:T(8,128)(2,1)S(1)} %get-tuple-element.169) | copy-start | bytes 3145732
  111.3 320.4 %reduce-scatter.7.cloned.1.call-start = ((), (), s32[]{:S(2)}) async-start(), calls=%async_computation.10 | async-start | bytes 2228224
  294.5 11.6 %copy-start.2 = (bf16[16,512,128]{1,2,0:T(8,128)(2,1)S(1)}, bf16[16,512,128]{1,2,0:T(8,128)(2,1)}, u32[]{:S(2)}) copy-start(bf16[16,512,128]{1,2,0:T(8,128)(2,1)} %copy-done.1) | copy-start | bytes 6291460
  315.6 117.2 %copy-start.15 = (bf16[512,128]{1,0:T(8,128)(2,1)S(1)}, bf16[512,128]{1,0:T(8,128)(2,1)}, u32[]{:S(2)}) copy-start(bf16[512,128]{1,0:T(8,128)(2,1)} %param.20) | copy-start | bytes 393220
  315.6 175.5 %all-gather.15.cloned.1.call-start = ((), (), s32[]{:S(2)}) async-start(), calls=%async_computation.7 | async-start | bytes 1310720 | tf_op jit(solution)/shard_map/all_gather | solution.py:181
  466.2 13.7 %copy-start = (bf16[16,512,128]{1,2,0:T(8,128)(2,1)}, bf16[16,512,128]{1,2,0:T(8,128)(2,1)S(1)}, u32[]{:S(2)}) copy-start(bf16[16,512,128]{1,2,0:T(8,128)(2,1)S(1)} %fusion.6) | copy-start | bytes 6291460
  468.7 47.0 %all-gather.13.cloned.1.call-start = ((), (), s32[]{:S(2)}) async-start(), calls=%async_computation.6 | async-start | bytes 1310720 | tf_op jit(solution)/shard_map/all_gather | solution.py:182
  469.4 3.8 collective-permute-start.1
  476.7 243.6 %all-gather.19.cloned.1.call-start = ((), (), s32[]{:S(2)}) async-start(), calls=%async_computation.9 | async-start | bytes 8912896 | tf_op jit(solution)/shard_map/all_gather | solution.py:25
  481.1 11.9 %copy-start.35 = (f32[1,1,4,1,256]{4,2,0,1,3:T(4,128)S(1)}, f32[1,1,4,1,256]{4,2,0,1,3:T(4,128)}, u32[]{:S(2)}) copy-start(f32[1,1,4,1,256]{4,2,0,1,3:T(4,128)} %copy.172) | copy-start | bytes 12292
  535.7 322.1 %reduce-scatter.9.cloned.1.call-start = ((), (), s32[]{:S(2)}) async-start(), calls=%async_computation.11 | async-start | bytes 2228224
  618.8 101.6 %copy-start.71 = (bf16[16]{0:T(256)(128)(2,1)S(1)}, bf16[16]{0:T(256)(128)(2,1)}, u32[]{:S(2)}) copy-start(bf16[16]{0:T(256)(128)(2,1)} %get-tuple-element.333) | copy-start | bytes 100
  742.8 280.4 %all-reduce.8.cloned.1.call-start = ((), (), s32[]{:S(2)}) async-start(), calls=%async_computation.12 | async-start | bytes 6291456 | tf_op jit(solution)/shard_map/psum | solution.py:44
  (61 other events, 210.0 us)
Sparse Core Ops, SparseCore 0:
  48.1 24.6 all-gather.10
  74.6 22.8 all-gather.8
  111.4 182.9 all-gather.16
  315.7 115.9 reduce-scatter.6
  468.8 22.3 all-gather.14
  492.8 22.8 all-gather.12
  535.8 184.5 all-gather.18
  743.0 114.7 reduce-scatter.8
  860.9 162.3 all-reduce.7
